TPU v7x, 512 devices: a whole 4x4x16 slice. The times are simulated.
512 devices in a mesh: row: 16 (over x, z_hi, core), col: 32 (over y, z_lo).
Axes of the slice: x: 4, y: 4, z: 16 (z_hi: 2, z_lo: 8; z = z_hi * 8 + z_lo), core: 2. Of those that a mesh axis runs over, the one named last changes fastest.
Arguments:
- tokens: bfloat16 [16384, 16384], P('row', 'col'), may hold values from -6 to 6
- up_weight: bfloat16 [16384, 28672], P('row', 'col'), may hold values from -0.125 to 0.125
Outputs:
- projected: bfloat16 [16384, 28672], P('row', 'col')
All inputs are finite; a program needn't handle non-finite values.
Results may differ from a plain program's by a relative error of at most 0.001.
Values may be sent and summed in bfloat16 or wider, within the bound.
A program may use at most 64 MiB of HBM per device.

v0:
```python
import jax
import jax.numpy as jnp
from jax import lax
from jax.sharding import PartitionSpec as P


def from_root(value, axis, source):
    kept = jnp.where(lax.axis_index(axis) == source, value, 0).astype(value.dtype)
    return lax.psum(kept, axis)


def from_behind(x, axis, by):
    count = lax.axis_size(axis)
    return lax.ppermute(x, axis, [(i, (i + by) % count) for i in range(count)])


def body(tokens, up_weight):
    row_index = lax.axis_index("row")
    col_count = lax.axis_size("col")
    pieces_list = []
    for position in range(4):
        pieces_list.append(from_root(tokens, "col", (2 * row_index + position) % col_count))
    gathered = jnp.concatenate(pieces_list, axis=1)
    split_at = up_weight.shape[0]
    own_part = jnp.dot(gathered[:, :split_at], up_weight, preferred_element_type=jnp.float32)
    following = from_behind(up_weight, "row", -1)
    next_part = jnp.dot(gathered[:, split_at:], following, preferred_element_type=jnp.float32)
    return (own_part + next_part).astype(jnp.bfloat16)


def solution(mesh):
    placed = (P("row", "col"), P("row", "col"))
    return jax.shard_map(
        body, mesh=mesh, in_specs=placed, out_specs=P("row", "col"), check_vma=False
    )
```

profile of v0, /device:TPU:2, one launch (start us, length us, event | category | flops | bytes accessed | tf_op | source)
XLA Modules:
  0.0 536.4 jit_solution(7711326817328430538)
XLA Ops:
  6.5 0.0 all-reduce.3.cloned.1.call-start
  6.5 3.4 broadcast_select_fusion.1
  9.9 0.0 copy-start
  9.9 0.0 all-reduce.3.cloned.1.call-update
  9.9 1.5 copy-done
  11.4 15.1 %collective-permute-start = (bf16[1024,896]{1,0:T(8,128)(2,1)S(1)}, bf16[1024,896]{1,0:T(8,128)(2,1)}, u32[]{:S(2)}, u32[]{:S(2)}) collective-permute-start(bf16[1024,896]{1,0:T(8,128)(2,1)S(1)} %copy-done), channel_id=1, source_target_pairs={{0,480},{32,0},{64,32},{96,64},{128,96},{160,128},{192,160},{224,1... | collective-permute-start | bytes 5505032 | tf_op jit(solution)/shard_map/ppermute | solution.py:14
  26.5 493.9 %all-reduce.3.cloned.1.call-done = (bf16[1024,512]{1,0:T(8,128)(2,1)}, bf16[1024,512]{1,0:T(8,128)(2,1)}, bf16[1024,512]{1,0:T(8,128)(2,1)}, bf16[1024,512]{1,0:T(8,128)(2,1)}) async-done(((bf16[1024,512]{1,0:T(8,128)(2,1)}, bf16[1024,512]{1,0:T(8,128)(2,1)}, bf16[1024,512]{1,0:T(8,128)(2,1)}, bf16[1024,512]{1,0:T(8,128)(2,1)}), (bf16[1024,512]{1,0:T(8,128)(2,1)}, bf16[1024,512]{1,0:T(8,128)(2,1)}, ...) | async-done | bytes 4194320 | tf_op jit(solution)/shard_map/psum | solution.py:9
  520.5 0.0 copy-start.1
  520.5 0.0 copy-start.2
  520.5 4.0 fusion
  524.5 0.0 collective-permute-done
  524.5 0.0 copy-done.1
  524.5 0.0 copy-done.2
  524.5 5.1 add_convert_fusion
Async XLA Ops:
  6.5 513.9 %all-reduce.3.cloned.1.call-start = ((), (), s32[]{:S(2)}) async-start(), calls=%async_computation | async-start | bytes 8388608 | tf_op jit(solution)/shard_map/psum | solution.py:9
  9.9 1.5 copy-start
  11.4 513.1 %collective-permute-start = (bf16[1024,896]{1,0:T(8,128)(2,1)S(1)}, bf16[1024,896]{1,0:T(8,128)(2,1)}, u32[]{:S(2)}, u32[]{:S(2)}) collective-permute-start(bf16[1024,896]{1,0:T(8,128)(2,1)S(1)} %copy-done), channel_id=1, source_target_pairs={{0,480},{32,0},{64,32},{96,64},{128,96},{160,128},{192,160},{224,1... | collective-permute-start | bytes 5505032 | tf_op jit(solution)/shard_map/ppermute | solution.py:14
  520.5 4.0 copy-start.1
  520.5 4.0 copy-start.2
Sparse Core Ops, SparseCore 0:
  10.5 509.9 all-reduce.2
where the time goes:
time: 537 us; the launch traced here: 536 us
  waiting for transfers between devices  494 us (92%)
  starting transfers between devices  15.1 us (3%)
  between operations  13.4 us (2%)
  matrix products  9.08 us (2%)
    psum x1, waiting for transfers between devices, from_root(): return lax.psum(kept, axis)  494 us
    ppermute x1, starting transfers between devices, from_behind(): return lax.ppermute(x, axis, [(i, (i + by) % count) for i in range(count)])  15.1 us
  transfers between devices with their start and end apart: 2, of which 1 were waited for; matrix products, arithmetic and copies ran while one was open for 1% of the time, Pallas kernels for 0%

commit v1 on v0

v1 whole, which is shorter than its diff:
```python
import jax
import jax.numpy as jnp
from jax import lax
from jax.experimental import pallas as pl
from jax.experimental.pallas import tpu as pltpu
from jax.sharding import PartitionSpec as P

MESH = pl.DeviceIdType.MESH
ROWS, COLS = 16, 32
NY, NZ = 4, 8
PIECES = 4
SUBS = 2
WCHUNKS = 4


def kernel(tok, w, out, gath, land, w_own, w_next, acc, obuf,
           own_sem, w_send, w_recv, land_sem, gath_sem, s1_send, z_send, y_send, out_sem):
    row = lax.axis_index("row")
    col = lax.axis_index("col")
    core = lax.rem(row, 2)
    even = row - core
    y = col // NZ
    z = lax.rem(col, NZ)
    tokens = tok.shape[0]
    quarter = tokens // NY
    sub = quarter // SUBS
    depth = w.shape[0]
    wrows = depth // WCHUNKS
    piece_cols = tok.shape[1]
    per_piece = depth // piece_cols

    def at(y_, z_):
        return lax.rem(y_ + NY, NY) * NZ + z_

    def signal(r_, c_):
        pl.semaphore_signal(barrier, inc=1, device_id=(r_, c_), device_id_type=MESH)

    def piece_of(a, p):
        c_ = lax.rem(2 * (even + a) + p, COLS)
        return c_ // NZ, lax.rem(c_, NZ)

    def loop(n, f):
        lax.fori_loop(0, n, lambda i, carry: (f(i), carry)[1], 0)

    def rows_of(q, j):
        return pl.ds(pl.multiple_of(q * quarter + j * sub, sub), sub)

    def remote(src, dst, send, recv, r_, c_):
        return pltpu.make_async_remote_copy(
            src_ref=src, dst_ref=dst, send_sem=send, recv_sem=recv,
            device_id=(r_, c_), device_id_type=MESH)

    mine = lax.rem(col - 2 * row + 2 * COLS, COLS)
    is_source = mine < PIECES

    own_copy = pltpu.make_async_copy(w, w_own, own_sem)
    own_copy.start()

    def own_part(j):
        return pltpu.make_async_copy(
            tok.at[rows_of(y, j)], gath.at[mine, rows_of(y, j)], land_sem.at[1, mine, j])

    @pl.when(jnp.logical_and(core == 1, is_source))
    def _():
        loop(SUBS, lambda j: own_part(j).start())

    barrier = pltpu.get_barrier_semaphore()
    behind = lax.rem(row + ROWS - 1, ROWS)
    ahead = lax.rem(row + 1, ROWS)

    @pl.when(core == 0)
    def _():
        for dy in range(NY):
            signal(row + 1, at(y + dy, z))
        pl.semaphore_wait(barrier, NY + 1)

    @pl.when(core == 1)
    def _():
        signal(ahead, col)

        @pl.when(z > 0)
        def _():
            signal(row, at(y, z - 1))

        @pl.when(z < NZ - 1)
        def _():
            signal(row, at(y, z + 1))

        for dy in range(1, NY):
            signal(row, at(y + dy, z))
        for dy in range(NY):
            signal(row - 1, at(y + dy, z))
        middle = jnp.logical_and(z > 0, z < NZ - 1)
        pl.semaphore_wait(barrier, 2 * NY + jnp.where(middle, 1, 0))

    def s1_from0(q, j):
        return remote(tok.at[rows_of(q, j)], land.at[mine, pl.ds(j * sub, sub)],
                      s1_send.at[q, j], land_sem.at[0, mine, j], even + 1, at(q, z))

    def s1_from1(q, j):
        return remote(tok.at[rows_of(q, j)], gath.at[mine, rows_of(q, j)],
                      s1_send.at[q, j], land_sem.at[1, mine, j], row, at(q, z))

    def each_s1(act):
        @pl.when(jnp.logical_and(core == 0, is_source))
        def _():
            loop(SUBS, lambda j: loop(NY, lambda q: act(s1_from0(q, j))))

        @pl.when(jnp.logical_and(core == 1, is_source))
        def _():
            def one(q, j):
                @pl.when(q != y)
                def _():
                    act(s1_from1(q, j))
            loop(SUBS, lambda j: loop(NY, lambda q: one(q, j)))

    each_s1(lambda copy: copy.start())

    def w_copy(k):
        part = pl.ds(pl.multiple_of(k * wrows, wrows), wrows)
        return remote(w.at[part], w_next.at[part], w_send.at[k], w_recv.at[k], behind, col)

    loop(WCHUNKS, lambda k: w_copy(k).start())

    def relay_src(a, p, j):
        return land.at[p, pl.ds(j * sub, sub)] if a == 0 else gath.at[p, rows_of(y, j)]

    def z_copy(a, p, j, up):
        ref = relay_src(a, p, j)
        return remote(ref, ref, z_send.at[a, p, j, up], land_sem.at[a, p, j],
                      row, at(y, z + 1 if up else z - 1))

    def y_copy(a, p, j, dy):
        return remote(relay_src(a, p, j), gath.at[p, rows_of(y, j)],
                      y_send.at[a, p, j, dy], gath_sem.at[p, y, j], even + a, at(y + dy, z))

    def sends(a, p, j, zp, act):
        @pl.when(jnp.logical_and(z >= zp, z < NZ - 1))
        def _():
            act(z_copy(a, p, j, 1))

        @pl.when(jnp.logical_and(z <= zp, z > 0))
        def _():
            act(z_copy(a, p, j, 0))

        for dy in ((1, 3, 2) if a == 1 else (1, 3, 2, 0)):
            act(y_copy(a, p, j, dy))

    def arrived(a, p, j):
        ref = relay_src(a, p, j)
        return pltpu.make_async_copy(ref, ref, land_sem.at[a, p, j])

    @pl.when(core == 1)
    def _():
        def step(s):
            for a in (0, 1):
                def one(p, a=a):
                    zp = piece_of(a, p)[1]

                    @pl.when(jnp.abs(z - zp) == s)
                    def _():
                        def part(j):
                            arrived(a, p, j).wait()
                            sends(a, p, j, zp, lambda copy: copy.start())
                        loop(SUBS, part)
                loop(PIECES, one)
        loop(NZ, step)

    def have(p):
        def one(q):
            @pl.when(jnp.logical_or(core == 0, q != y))
            def _():
                def part(j):
                    ref = gath.at[p, rows_of(q, j)]
                    pltpu.make_async_copy(ref, ref, gath_sem.at[p, q, j]).wait()
                loop(SUBS, part)
        loop(NY, one)

    def q_rows(q):
        return pl.ds(pl.multiple_of(q * quarter, quarter), quarter)

    own_copy.wait()
    for p in range(per_piece):
        have(p)

    def first(q):
        total = jnp.dot(gath[0, q_rows(q)], w_own[:piece_cols], preferred_element_type=jnp.float32)
        for p in range(1, per_piece):
            total += jnp.dot(gath[p, q_rows(q)], w_own[p * piece_cols:(p + 1) * piece_cols],
                             preferred_element_type=jnp.float32)
        acc[q_rows(q)] = total
    loop(NY, first)

    def out_copy(q):
        return pltpu.make_async_copy(obuf.at[q_rows(q)], out.at[q_rows(q)], out_sem.at[q])

    for p in range(per_piece, PIECES):
        have(p)
    for k in range(WCHUNKS):
        w_copy(k).wait_recv()
        p = per_piece + k * wrows // piece_cols
        c0 = k * wrows % piece_cols

        def more(q):
            total = acc[q_rows(q)] + jnp.dot(
                gath[p, q_rows(q), c0:c0 + wrows], w_next[k * wrows:(k + 1) * wrows],
                preferred_element_type=jnp.float32)
            if k < WCHUNKS - 1:
                acc[q_rows(q)] = total
            else:
                obuf[q_rows(q)] = total.astype(obuf.dtype)
                out_copy(q).start()
        loop(NY, more)

    loop(NY, lambda q: out_copy(q).wait())
    loop(WCHUNKS, lambda k: w_copy(k).wait_send())
    each_s1(lambda copy: copy.wait_send())

    @pl.when(core == 1)
    def _():
        for a in (0, 1):
            def one(p, a=a):
                zp = piece_of(a, p)[1]
                loop(SUBS, lambda j: sends(a, p, j, zp, lambda copy: copy.wait_send()))
            loop(PIECES, one)


def body(tokens, up_weight):
    rows, cols = tokens.shape
    depth, width = up_weight.shape
    hbm = pl.BlockSpec(memory_space=pl.ANY)
    dma = pltpu.SemaphoreType.DMA
    bf16 = jnp.bfloat16
    return pl.pallas_call(
        kernel,
        out_shape=jax.ShapeDtypeStruct((rows, width), bf16),
        in_specs=[hbm, hbm],
        out_specs=hbm,
        scratch_shapes=[
            pltpu.VMEM((PIECES, rows, cols), bf16),
            pltpu.VMEM((PIECES, rows // NY, cols), bf16),
            pltpu.VMEM((depth, width), bf16),
            pltpu.VMEM((depth, width), bf16),
            pltpu.VMEM((rows, width), jnp.float32),
            pltpu.VMEM((rows, width), bf16),
            dma, dma((WCHUNKS,)), dma((WCHUNKS,)),
            dma((2, PIECES, SUBS)), dma((PIECES, NY, SUBS)), dma((NY, SUBS)),
            dma((2, PIECES, SUBS, 2)), dma((2, PIECES, SUBS, NY)), dma((NY,)),
        ],
        compiler_params=pltpu.CompilerParams(collective_id=0, has_side_effects=True),
        name="banded",
    )(tokens, up_weight)


def solution(mesh):
    placed = (P("row", "col"), P("row", "col"))
    return jax.shard_map(
        body, mesh=mesh, in_specs=placed, out_specs=P("row", "col"), check_vma=False
    )
```

time: 537 us -> 142 us (0.26)
  the two profiles are of different devices: /device:TPU:2 before, /device:TPU:226 now
where the time goes in v1:
time: 142 us
  Pallas kernels  139 us (98%)
  local copies, waits for them, and re-layouts  2.87 us (2%)
    pallas_call x1, Pallas kernels, body(): pl.pallas_call(kernel, out_shape=jax.ShapeDtypeStruct((rows, width), bf16...  139 us
    unnamed x1, local copies, waits for them, and re-layouts  2.87 us

profile of v1, /device:TPU:226, one launch (start us, length us, event | category | flops | bytes accessed | tf_op | source)
XLA Modules:
  0.0 142.1 jit_solution(748863699387124231)
XLA Ops:
  0.0 139.3 %banded.1 = bf16[1024,896]{1,0:T(8,128)(2,1)} custom-call(bf16[1024,512]{1,0:T(8,128)(2,1)} %tok.1, bf16[1024,896]{1,0:T(8,128)(2,1)} %w.1), custom_call_target="tpu_custom_call" | custom-call | tf_op jit(solution)/shard_map/banded/pallas_call | solution.py:234
  139.3 2.9 %copy.4 = bf16[1024,896]{1,0:T(8,128)(2,1)} copy(bf16[1024,896]{1,0:T(8,128)(2,1)} %banded.1) | data formatting | bytes 3670016

commit v2 on v1

--- a/solution.py
+++ b/solution.py
@@ -10,11 +10,13 @@
 NY, NZ = 4, 8
 PIECES = 4
 SUBS = 2
-WCHUNKS = 4
-
-
-def kernel(tok, w, out, gath, land, w_own, w_next, acc, obuf,
-           own_sem, w_send, w_recv, land_sem, gath_sem, s1_send, z_send, y_send, out_sem):
+WCHUNKS = 8
+HOPS = 8
+NX, RING = 4, 16
+
+
+def kernel(tok, w, out, gath, land, w_own, w_next, acc, obuf, held,
+           own_sem, pair_send, pair_recv, f_send, h_send, h_recv, w_recv, land_sem, gath_sem, s1_send, z_send, y_send, out_sem):
     row = lax.axis_index("row")
     col = lax.axis_index("col")
     core = lax.rem(row, 2)
@@ -25,7 +27,8 @@
     quarter = tokens // NY
     sub = quarter // SUBS
     depth = w.shape[0]
-    wrows = depth // WCHUNKS
+    half = depth // 2
+    wrows = half // WCHUNKS
     piece_cols = tok.shape[1]
     per_piece = depth // piece_cols
 
@@ -64,19 +67,33 @@
     def _():
         loop(SUBS, lambda j: own_part(j).start())
 
+    x = row // (ROWS // NX)
+    ring = NZ * lax.rem(row // 2, 2) + z
+    near = (lax.rem(ring + 1, RING), lax.rem(ring + RING - 1, RING))
+
+    def chip(x_, ring_, core_):
+        return (x_ * 2 + ring_ // NZ) * 2 + core_, y * NZ + lax.rem(ring_, NZ)
+
+    def x_from(ring_):
+        return lax.rem(x + NX + jnp.where(ring_ < NZ, 1, 0), NX)
+
+    x_to = lax.rem(x + NX - jnp.where(ring < NZ, 1, 0), NX)
+
     barrier = pltpu.get_barrier_semaphore()
-    behind = lax.rem(row + ROWS - 1, ROWS)
-    ahead = lax.rem(row + 1, ROWS)
 
     @pl.when(core == 0)
     def _():
+        for n_ in near:
+            signal(*chip(x_from(n_), n_, 0))
+            signal(*chip(x, n_, 0))
         for dy in range(NY):
             signal(row + 1, at(y + dy, z))
-        pl.semaphore_wait(barrier, NY + 1)
-
-    @pl.when(core == 1)
-    def _():
-        signal(ahead, col)
+        pl.semaphore_wait(barrier, NY + 6)
+
+    @pl.when(core == 1)
+    def _():
+        for n_ in near:
+            signal(*chip(x, n_, 0))
 
         @pl.when(z > 0)
         def _():
@@ -116,11 +133,35 @@
 
     each_s1(lambda copy: copy.start())
 
-    def w_copy(k):
-        part = pl.ds(pl.multiple_of(k * wrows, wrows), wrows)
-        return remote(w.at[part], w_next.at[part], w_send.at[k], w_recv.at[k], behind, col)
-
-    loop(WCHUNKS, lambda k: w_copy(k).start())
+    def pair_copy():
+        return remote(w, w_next, pair_send, pair_recv, even, col)
+
+    def w_part(d, j):
+        return pl.ds(pl.multiple_of(d * half + j * wrows, wrows), wrows)
+
+    def first_hop(d, j):
+        return remote(w.at[w_part(d, j)], held.at[d, 0, j], f_send.at[d, j], h_recv.at[d, 0, j],
+                      *chip(x_to, near[d], 0))
+
+    def next_hop(d, h, j):
+        return remote(held.at[d, h - 1, j], held.at[d, h, j], h_send.at[d, h, j], h_recv.at[d, h, j],
+                      *chip(x, near[d], 0))
+
+    def last_hop(d, j):
+        return remote(held.at[d, HOPS - 2, j], w_next.at[w_part(d, j)],
+                      h_send.at[d, HOPS - 1, j], w_recv.at[d, j], *chip(x, near[d], 1))
+
+    def held_in(d, h, j):
+        ref = held.at[d, h, j]
+        return pltpu.make_async_copy(ref, ref, h_recv.at[d, h, j])
+
+    @pl.when(core == 1)
+    def _():
+        pair_copy().start()
+
+    @pl.when(core == 0)
+    def _():
+        loop(WCHUNKS, lambda j: (first_hop(0, j).start(), first_hop(1, j).start()))
 
     def relay_src(a, p, j):
         return land.at[p, pl.ds(j * sub, sub)] if a == 0 else gath.at[p, rows_of(y, j)]
@@ -179,41 +220,96 @@
     def q_rows(q):
         return pl.ds(pl.multiple_of(q * quarter, quarter), quarter)
 
-    own_copy.wait()
-    for p in range(per_piece):
-        have(p)
-
-    def first(q):
-        total = jnp.dot(gath[0, q_rows(q)], w_own[:piece_cols], preferred_element_type=jnp.float32)
-        for p in range(1, per_piece):
-            total += jnp.dot(gath[p, q_rows(q)], w_own[p * piece_cols:(p + 1) * piece_cols],
-                             preferred_element_type=jnp.float32)
-        acc[q_rows(q)] = total
-    loop(NY, first)
-
     def out_copy(q):
         return pltpu.make_async_copy(obuf.at[q_rows(q)], out.at[q_rows(q)], out_sem.at[q])
 
-    for p in range(per_piece, PIECES):
-        have(p)
-    for k in range(WCHUNKS):
-        w_copy(k).wait_recv()
-        p = per_piece + k * wrows // piece_cols
-        c0 = k * wrows % piece_cols
-
-        def more(q):
-            total = acc[q_rows(q)] + jnp.dot(
-                gath[p, q_rows(q), c0:c0 + wrows], w_next[k * wrows:(k + 1) * wrows],
-                preferred_element_type=jnp.float32)
-            if k < WCHUNKS - 1:
-                acc[q_rows(q)] = total
-            else:
-                obuf[q_rows(q)] = total.astype(obuf.dtype)
-                out_copy(q).start()
-        loop(NY, more)
+    def product(p, q, weights, r0, rows):
+        c0 = r0 % piece_cols
+        return jnp.dot(gath[p, q_rows(q), c0:c0 + rows], weights[r0:r0 + rows],
+                       preferred_element_type=jnp.float32)
+
+    def own_product(q):
+        total = product(0, q, w_own, 0, piece_cols)
+        for p in range(1, per_piece):
+            total += product(p, q, w_own, p * piece_cols, piece_cols)
+        return total
+
+    @pl.when(core == 0)
+    def _():
+        def pass_on(h):
+            def one(j):
+                for d in (0, 1):
+                    held_in(d, h - 1, j).wait()
+                    next_hop(d, h, j).start()
+            loop(WCHUNKS, one)
+        lax.fori_loop(1, HOPS - 1, lambda h, c: (pass_on(h), c)[1], 0)
+
+        def finish(j):
+            for d in (0, 1):
+                held_in(d, HOPS - 2, j).wait()
+                last_hop(d, j).start()
+        loop(WCHUNKS, finish)
+
+        own_copy.wait()
+        pair_copy().wait_recv()
+        for p in range(PIECES):
+            have(p)
+
+        def whole(q):
+            total = own_product(q)
+            for p in range(per_piece, PIECES):
+                total += product(p, q, w_next, (p - per_piece) * piece_cols, piece_cols)
+            obuf[q_rows(q)] = total.astype(obuf.dtype)
+            out_copy(q).start()
+        loop(NY, whole)
+
+    @pl.when(core == 1)
+    def _():
+        own_copy.wait()
+        for p in range(PIECES):
+            have(p)
+
+        def begin(q):
+            acc[q_rows(q)] = own_product(q)
+        loop(NY, begin)
+
+        groups = 2
+        for g in range(groups):
+            span = half // groups
+
+            def got(j):
+                for d in (0, 1):
+                    ref = w_next.at[w_part(d, j)]
+                    pltpu.make_async_copy(ref, ref, w_recv.at[d, j]).wait()
+            lax.fori_loop(g * WCHUNKS // groups, (g + 1) * WCHUNKS // groups, lambda j, c: (got(j), c)[1], 0)
+
+            def more(q):
+                total = acc[q_rows(q)]
+                for d in (0, 1):
+                    r0 = d * half + g * span
+                    total += product(per_piece + r0 // piece_cols, q, w_next, r0, span)
+                if g < groups - 1:
+                    acc[q_rows(q)] = total
+                else:
+                    obuf[q_rows(q)] = total.astype(obuf.dtype)
+                    out_copy(q).start()
+            loop(NY, more)
 
     loop(NY, lambda q: out_copy(q).wait())
-    loop(WCHUNKS, lambda k: w_copy(k).wait_send())
+
+    @pl.when(core == 0)
+    def _():
+        def sent(j):
+            for d in (0, 1):
+                first_hop(d, j).wait_send()
+                lax.fori_loop(1, HOPS - 1, lambda h, c: (next_hop(d, h, j).wait_send(), c)[1], 0)
+                last_hop(d, j).wait_send()
+        loop(WCHUNKS, sent)
+
+    @pl.when(core == 1)
+    def _():
+        pair_copy().wait_send()
+
     each_s1(lambda copy: copy.wait_send())
 
     @pl.when(core == 1)
@@ -243,7 +339,9 @@
             pltpu.VMEM((depth, width), bf16),
             pltpu.VMEM((rows, width), jnp.float32),
             pltpu.VMEM((rows, width), bf16),
-            dma, dma((WCHUNKS,)), dma((WCHUNKS,)),
+            pltpu.VMEM((2, HOPS - 1, WCHUNKS, depth // (2 * WCHUNKS), width), bf16),
+            dma, dma, dma, dma((2, WCHUNKS)), dma((2, HOPS, WCHUNKS)), dma((2, HOPS - 1, WCHUNKS)),
+            dma((2, WCHUNKS)),
             dma((2, PIECES, SUBS)), dma((PIECES, NY, SUBS)), dma((NY, SUBS)),
             dma((2, PIECES, SUBS, 2)), dma((2, PIECES, SUBS, NY)), dma((NY,)),
         ],

time: 142 us -> 119 us (0.84)
  the two profiles are of different devices: /device:TPU:226 before, /device:TPU:29 now
where the time goes in v2:
time: 119 us
  Pallas kernels  116 us (97%)
  local copies, waits for them, and re-layouts  2.87 us (2%)
    pallas_call x1, Pallas kernels, body(): pl.pallas_call(kernel, out_shape=jax.ShapeDtypeStruct((rows, width), bf16...  116 us
    unnamed x1, local copies, waits for them, and re-layouts  2.87 us

profile of v2, /device:TPU:29, one launch (start us, length us, event | category | flops | bytes accessed | tf_op | source)
XLA Modules:
  0.0 119.2 jit_solution(9372898335655444368)
XLA Ops:
  0.0 116.3 %banded.1 = bf16[1024,896]{1,0:T(8,128)(2,1)} custom-call(bf16[1024,512]{1,0:T(8,128)(2,1)} %tok.1, bf16[1024,896]{1,0:T(8,128)(2,1)} %w.1), custom_call_target="tpu_custom_call" | custom-call | tf_op jit(solution)/shard_map/banded/pallas_call | solution.py:330
  116.3 2.9 %copy.4 = bf16[1024,896]{1,0:T(8,128)(2,1)} copy(bf16[1024,896]{1,0:T(8,128)(2,1)} %banded.1) | data formatting | bytes 3670016

commit v3 on v2

--- a/solution.py
+++ b/solution.py
@@ -15,8 +15,8 @@
 NX, RING = 4, 16
 
 
-def kernel(tok, w, out, gath, land, w_own, w_next, acc, obuf, held,
-           own_sem, pair_send, pair_recv, f_send, h_send, h_recv, w_recv, land_sem, gath_sem, s1_send, z_send, y_send, out_sem):
+def kernel(tok, w, out, gath, land, w_own, w_next, acc, held,
+           own_sem, pair_send, pair_recv, f_send, h_send, h_recv, w_recv, land_sem, gath_sem, s1_send, z_send, y_send):
     row = lax.axis_index("row")
     col = lax.axis_index("col")
     core = lax.rem(row, 2)
@@ -220,9 +220,6 @@
     def q_rows(q):
         return pl.ds(pl.multiple_of(q * quarter, quarter), quarter)
 
-    def out_copy(q):
-        return pltpu.make_async_copy(obuf.at[q_rows(q)], out.at[q_rows(q)], out_sem.at[q])
-
     def product(p, q, weights, r0, rows):
         c0 = r0 % piece_cols
         return jnp.dot(gath[p, q_rows(q), c0:c0 + rows], weights[r0:r0 + rows],
@@ -259,8 +256,7 @@
             total = own_product(q)
             for p in range(per_piece, PIECES):
                 total += product(p, q, w_next, (p - per_piece) * piece_cols, piece_cols)
-            obuf[q_rows(q)] = total.astype(obuf.dtype)
-            out_copy(q).start()
+            out[q_rows(q)] = total.astype(out.dtype)
         loop(NY, whole)
 
     @pl.when(core == 1)
@@ -291,11 +287,9 @@
                 if g < groups - 1:
                     acc[q_rows(q)] = total
                 else:
-                    obuf[q_rows(q)] = total.astype(obuf.dtype)
-                    out_copy(q).start()
+                    out[q_rows(q)] = total.astype(out.dtype)
             loop(NY, more)
 
-    loop(NY, lambda q: out_copy(q).wait())
 
     @pl.when(core == 0)
     def _():
@@ -327,25 +321,26 @@
     hbm = pl.BlockSpec(memory_space=pl.ANY)
     dma = pltpu.SemaphoreType.DMA
     bf16 = jnp.bfloat16
+    tokens = pltpu.with_memory_space_constraint(tokens, pltpu.HBM)
+    up_weight = pltpu.with_memory_space_constraint(up_weight, pltpu.HBM)
     return pl.pallas_call(
         kernel,
         out_shape=jax.ShapeDtypeStruct((rows, width), bf16),
-        in_specs=[hbm, hbm],
-        out_specs=hbm,
+        in_specs=[pl.BlockSpec(memory_space=pltpu.HBM)] * 2,
+        out_specs=pl.BlockSpec(memory_space=pltpu.VMEM),
         scratch_shapes=[
             pltpu.VMEM((PIECES, rows, cols), bf16),
             pltpu.VMEM((PIECES, rows // NY, cols), bf16),
             pltpu.VMEM((depth, width), bf16),
             pltpu.VMEM((depth, width), bf16),
             pltpu.VMEM((rows, width), jnp.float32),
-            pltpu.VMEM((rows, width), bf16),
             pltpu.VMEM((2, HOPS - 1, WCHUNKS, depth // (2 * WCHUNKS), width), bf16),
             dma, dma, dma, dma((2, WCHUNKS)), dma((2, HOPS, WCHUNKS)), dma((2, HOPS - 1, WCHUNKS)),
             dma((2, WCHUNKS)),
             dma((2, PIECES, SUBS)), dma((PIECES, NY, SUBS)), dma((NY, SUBS)),
-            dma((2, PIECES, SUBS, 2)), dma((2, PIECES, SUBS, NY)), dma((NY,)),
+            dma((2, PIECES, SUBS, 2)), dma((2, PIECES, SUBS, NY)),
         ],
-        compiler_params=pltpu.CompilerParams(collective_id=0, has_side_effects=True),
+        compiler_params=pltpu.CompilerParams(collective_id=0, has_side_effects=True, vmem_limit_bytes=32<<20),
         name="banded",
     )(tokens, up_weight)
 

time: 119 us -> 117 us (0.983)
  local copies, waits for them, and re-layouts: 2.87 us -> 1.23 us
    unnamed x1, local copies, waits for them, and re-layouts: 2.87 us -> 1.23 us
where the time goes in v3:
time: 117 us
  Pallas kernels  115 us (98%)
  local copies, waits for them, and re-layouts  1.23 us (1%)
    pallas_call x1, Pallas kernels, body(): pl.pallas_call(kernel, out_shape=jax.ShapeDtypeStruct((rows, width), bf16...  115 us

profile of v3, /device:TPU:29, one launch (start us, length us, event | category | flops | bytes accessed | tf_op | source)
XLA Modules:
  0.0 116.7 jit_solution(3672644141243942201)
XLA Ops:
  0.0 115.5 %banded.1 = bf16[1024,896]{1,0:T(8,128)(2,1)S(1)} custom-call(bf16[1024,512]{1,0:T(8,128)(2,1)} %tok.1, bf16[1024,896]{1,0:T(8,128)(2,1)} %w.1), custom_call_target="tpu_custom_call" | custom-call | tf_op jit(solution)/shard_map/banded/pallas_call | solution.py:326
  115.5 1.2 %copy.4 = bf16[1024,896]{1,0:T(8,128)(2,1)} copy(bf16[1024,896]{1,0:T(8,128)(2,1)S(1)} %banded.1) | data formatting | bytes 3670016
